TPU v7x, 32 devices: a whole 2x2x4 slice. The times are simulated.
32 devices in a mesh: ens: 2 (over y), grid: 16 (over z, x, core).
Axes of the slice: x: 2, y: 2, z: 4, core: 2. Of those that a mesh axis runs over, the one named last changes fastest.
Arguments:
- fields: bfloat16 [2, 384, 768, 256], P('ens', 'grid'), may hold values from -6 to 6
- mode_counts: int32 [384], P('grid'), may hold values from 96 to 384, as said below
- gain_attn: float32 [256], replicated, may hold values from 0.5 to 1.5
- w_query: bfloat16 [256, 256], replicated, may hold values from -1 to 1
- w_key: bfloat16 [256, 256], replicated, may hold values from -8 to 8
- w_value: bfloat16 [256, 256], replicated, may hold values from -0.375 to 0.375
- w_out: bfloat16 [256, 256], replicated, may hold values from -0.375 to 0.375
- gain_spec: float32 [256], replicated, may hold values from 0.5 to 1.5
- w_first: bfloat16 [2, 8, 32, 32], replicated, may hold values from -1 to 1
- w_second: bfloat16 [2, 8, 32, 32], replicated, may hold values from -1 to 1
Outputs:
- layer_out: bfloat16 [2, 384, 768, 256], P('ens', 'grid')
Inputs may be any that keep to these rules, and one draw needn't show every extreme that they name: `mode_counts`: longitude wavenumbers kept in each latitude row; some row keeps all 384.
All inputs are finite; a program needn't handle non-finite values.
Results may differ from a plain program's by a relative error of at most 0.012.
Values may be sent and summed in bfloat16 or wider, within the bound.
A program may use at most 256 MiB of HBM per device.

v0:
```python
import math
import jax
import jax.numpy as jnp
from jax import lax
from jax.sharding import PartitionSpec as P

HEAD = 32
NLAT = 384
KLON = 384
KLAT = 128
norm_eps = 1e-05


def layer_norm(inputs, gain_vec):
    widened = inputs.astype(jnp.float32)
    center = widened - jnp.mean(widened, axis=-1, keepdims=True)
    spread = jnp.mean(center * center, axis=-1, keepdims=True)
    return center * lax.rsqrt(spread + norm_eps) * gain_vec


def lon_table(points, mode_count):
    positions = jnp.arange(points, dtype=jnp.int32)
    frequency = jnp.arange(mode_count, dtype=jnp.int32)
    turn_count = positions[:, None] * frequency[None, :] % points
    angles = 2.0 * math.pi / points * turn_count.astype(jnp.float32)
    factor = 1.0 / math.sqrt(points)
    return jnp.concatenate([jnp.cos(angles) * factor, -jnp.sin(angles) * factor], axis=1).astype(
        jnp.bfloat16
    )


def lon_inverse(points, mode_count):
    positions = jnp.arange(points, dtype=jnp.int32)
    frequency = jnp.arange(mode_count, dtype=jnp.int32)
    turn_count = frequency[:, None] * positions[None, :] % points
    angles = 2.0 * math.pi / points * turn_count.astype(jnp.float32)
    weight = jnp.where(frequency == 0, 1.0, 2.0).astype(jnp.float32)[:, None] / math.sqrt(points)
    return jnp.stack([jnp.cos(angles) * weight, -jnp.sin(angles) * weight]).astype(jnp.bfloat16)


def lat_angles(row_count, mode_count):
    frequency = jnp.arange(mode_count, dtype=jnp.int32)
    frequency = jnp.where(frequency < mode_count // 2, frequency, frequency - mode_count)
    positions = jnp.arange(row_count, dtype=jnp.int32)
    turn_count = frequency[:, None] * positions[None, :] % row_count
    return 2.0 * math.pi / row_count * turn_count.astype(jnp.float32)


def lat_forward(row_count, mode_count):
    angles = lat_angles(row_count, mode_count)
    factor = 1.0 / math.sqrt(row_count)
    cosine = jnp.cos(angles) * factor
    sine_part = jnp.sin(angles) * factor
    return jnp.stack(
        [jnp.stack([cosine, sine_part], axis=1), jnp.stack([-sine_part, cosine], axis=1)]
    ).astype(jnp.bfloat16)


def lat_inverse(row_count, mode_count):
    angles = jnp.transpose(lat_angles(row_count, mode_count))
    factor = 1.0 / math.sqrt(row_count)
    cosine = jnp.cos(angles) * factor
    sine_part = jnp.sin(angles) * factor
    return jnp.stack([jnp.stack([cosine, -sine_part]), jnp.stack([sine_part, cosine])]).astype(
        jnp.bfloat16
    )


def complex_blocks(weight):
    real_part = weight[0]
    imag_part = weight[1]
    return jnp.stack([jnp.stack([real_part, imag_part]), jnp.stack([-imag_part, real_part])])


def mix_blocks(spec, big):
    blocks = spec.reshape(spec.shape[:4] + (big.shape[2], big.shape[3]))
    out_blocks = jnp.einsum("mpqkbi,psbio->msqkbo", blocks, big, preferred_element_type=jnp.float32)
    return out_blocks.reshape(spec.shape)


def mix_members(all_scores, all_values, head_count):
    members, lat_rows, lon_points, feat_dim = all_values.shape
    row_max = jnp.max(all_scores, axis=0, keepdims=True)
    exps = jnp.exp(all_scores - row_max)
    totals = jnp.sum(exps, axis=0)
    weights = exps.astype(jnp.bfloat16)
    split_values = all_values.reshape(members, lat_rows, lon_points, head_count, HEAD)
    mixed_out = jnp.einsum(
        "nmlhw,nlwhe->mlwhe", weights, split_values, preferred_element_type=jnp.float32
    )
    mixed_out = mixed_out / jnp.transpose(totals, (0, 1, 3, 2))[..., None]
    return mixed_out.astype(jnp.bfloat16).reshape(
        all_scores.shape[1], lat_rows, lon_points, feat_dim
    )


def shards(
    fields, mode_counts, gain_attn, w_query, w_key, w_value, w_out, gain_spec, w_first, w_second
):
    mem_dev, lat_dev, lon_points, feat_dim = fields.shape
    head_count = feat_dim // HEAD
    score_scale = 1.0 / math.sqrt(HEAD)
    normed = layer_norm(fields, gain_attn).astype(jnp.bfloat16)
    queries = jnp.dot(normed, w_query, preferred_element_type=jnp.float32).astype(jnp.bfloat16)
    queries = queries.reshape(mem_dev, lat_dev, lon_points, head_count, HEAD)
    own_keys = jnp.dot(normed, w_key, preferred_element_type=jnp.float32).astype(jnp.bfloat16)
    own_values = jnp.dot(normed, w_value, preferred_element_type=jnp.float32).astype(jnp.bfloat16)
    key_rows = lax.all_gather(own_keys, "ens", axis=0, tiled=True)
    split_keys = key_rows.reshape(key_rows.shape[:3] + (head_count, HEAD))
    scores = (
        jnp.einsum("mlwhe,nlwhe->nmlhw", queries, split_keys, preferred_element_type=jnp.float32)
        * score_scale
    )
    all_values = lax.all_gather(own_values, "ens", axis=0, tiled=True)
    mixed_out = mix_members(scores, all_values, head_count)
    attended = (
        fields.astype(jnp.float32) + jnp.dot(mixed_out, w_out, preferred_element_type=jnp.float32)
    ).astype(jnp.bfloat16)
    retained = (jnp.arange(KLON, dtype=jnp.int32)[None, :] < mode_counts[:, None]).astype(
        jnp.float32
    )
    normed_two = layer_norm(attended, gain_spec).astype(jnp.bfloat16)
    spectrum = jnp.einsum(
        "mlxd,xk->mlkd", normed_two, lon_table(lon_points, KLON), preferred_element_type=jnp.float32
    )
    spectrum = spectrum.reshape(mem_dev, lat_dev, 2, KLON, feat_dim)
    spectrum = (spectrum * retained[None, :, None, :, None]).astype(jnp.bfloat16)
    forward = lat_forward(NLAT, KLAT)
    inverse = lat_inverse(NLAT, KLAT)
    big_one = complex_blocks(w_first)
    big_two = complex_blocks(w_second)
    rows_spec = jnp.einsum(
        "pqrj,mjrkd->mpqkd",
        forward,
        lax.all_to_all(spectrum, "grid", split_axis=3, concat_axis=1, tiled=True),
        preferred_element_type=jnp.float32,
    ).astype(jnp.bfloat16)
    hidden = jnp.maximum(mix_blocks(rows_spec, big_one), 0.0).astype(jnp.bfloat16)
    second = mix_blocks(hidden, big_two).astype(jnp.bfloat16)
    back_rows = jnp.einsum(
        "rpjq,mpqkd->mjrkd", inverse, second, preferred_element_type=jnp.float32
    ).astype(jnp.bfloat16)
    returned = lax.all_to_all(back_rows, "grid", split_axis=1, concat_axis=3, tiled=True)
    returned = returned * retained.astype(jnp.bfloat16)[None, :, None, :, None]
    field_out = jnp.einsum(
        "mjrkd,rkx->mjxd",
        returned,
        lon_inverse(lon_points, KLON),
        preferred_element_type=jnp.float32,
    )
    return (attended.astype(jnp.float32) + field_out).astype(jnp.bfloat16)


def solution(mesh):
    in_specs = (P("ens", "grid", None, None), P("grid"), P(), P(), P(), P(), P(), P(), P(), P())
    out_specs = P("ens", "grid", None, None)
    return jax.shard_map(shards, mesh=mesh, in_specs=in_specs, out_specs=out_specs, check_vma=False)
```

profile of v0, /device:TPU:11, one launch (start us, length us, event | category | flops | bytes accessed | tf_op | source)
XLA Modules:
  0.0 1163.1 jit_solution(6597510635387888419)
XLA Ops:
  6.5 0.0 copy-start
  6.5 0.0 all-gather.7.cloned.1.call-start
  6.5 12.6 %copy.142 = bf16[1,24,768,256]{2,3,1,0:T(8,128)(2,1)} copy(bf16[1,24,768,256]{3,2,1,0:T(8,128)(2,1)} %param.10) | data formatting | bytes 18874368 | tf_op args[0]
  19.2 0.0 copy-start.2
  19.2 5.2 convert_reduce_fusion.1
  24.4 1.2 copy-done.2
  25.5 2.6 fusion.7
  28.2 0.0 copy-done.8
  28.2 0.0 copy-done.10
  28.2 11.0 convolution_convert_fusion.1
  39.2 0.0 all-gather.7.cloned.1.call-update
  39.2 0.0 all-gather.5.cloned.1.call-start
  39.2 0.8 copy-done.11
  40.1 13.7 %convolution_convert_fusion.2 = bf16[24,768,256]{2,1,0:T(8,128)(2,1)} fusion(bf16[256,256]{1,0:T(8,128)(2,1)S(1)} %copy-done.11, bf16[1,24,768,256]{2,3,1,0:T(8,128)(2,1)} %copy.142, f32[256]{0:T(256)S(1)} %copy-done.8, f32[24,768]{1,0:T(8,128)S(1)} %add_rsqrt_fusion.1, f32[24,768]{1,0:T(8,128)S(1)} %broadcast_multiply_fusion.1), kind=kOutput, calls=%fused_computation.36 | convolution fusion | flops 2444230656 | bytes 19153920 | tf_op jit(solution)/shard_map/dot_general | solution.py:107
  53.8 0.0 all-gather.5.cloned.1.call-update
  53.8 5.3 multiply_convert_fusion.1
  59.1 0.0 copy-done.9
  59.1 0.7 fusion.85
  59.8 0.0 copy-done.4
  59.8 15.2 %bitcast_convert_fusion.3 = f32[24,8,768,32]{2,3,1,0:T(8,128)} fusion(bf16[256,256]{1,0:T(8,128)(2,1)S(1)} %copy-done.4, bf16[1,24,768,256]{2,3,1,0:T(8,128)(2,1)} %copy.142, f32[256]{0:T(256)S(1)} %copy-done.8, f32[24,768]{1,0:T(8,128)S(1)} %add_rsqrt_fusion.1, f32[24,768]{1,0:T(8,128)S(1)} %broadcast_multiply_fusion.1), kind=kOutput, calls=%fused_computation.143 | convolution fusion | flops 2448949248 | bytes 28591104 | tf_op jit(solution)/shard_map/dot_general | solution.py:104
  75.0 189.7 %all-gather.7.cloned.1.call-done = bf16[48,768,256]{2,1,0:T(8,128)(2,1)} async-done(((bf16[24,768,256]{2,1,0:T(8,128)(2,1)}), bf16[48,768,256]{2,1,0:T(8,128)(2,1)}) %all-gather.7.cloned.1.call-update) | async-done | bytes 18874384 | tf_op jit(solution)/shard_map/all_gather | solution.py:108
  264.7 24.2 %copy.207 = bf16[48,768,256]{1,2,0:T(8,128)(2,1)} copy(bf16[48,768,256]{2,1,0:T(8,128)(2,1)} %all-gather.7.cloned.1.call-done) | data formatting | bytes 37748736
  288.9 17.8 %multiply_reduce_fusion.1 = f32[24,8,768,2]{2,1,0,3:T(8,128)S(1)} fusion(bf16[24,8,768,32,2]{2,3,1,0,4:T(8,128)(2,1)} %bitcast.170, f32[24,8,768,32]{2,3,1,0:T(8,128)} %bitcast_convert_fusion.3), kind=kLoop, calls=%fused_computation.1 | loop fusion | flops 28016640 | bytes 38928384
  306.7 0.1 bitcast_reduce_fusion
  306.8 0.2 fusion.56
  307.1 183.5 %all-gather.5.cloned.1.call-done = bf16[48,768,256]{2,1,0:T(8,128)(2,1)} async-done(((bf16[24,768,256]{2,1,0:T(8,128)(2,1)}), bf16[48,768,256]{2,1,0:T(8,128)(2,1)}) %all-gather.5.cloned.1.call-update) | async-done | bytes 18874384 | tf_op jit(solution)/shard_map/all_gather | solution.py:114
  490.6 24.6 %copy.206 = bf16[48,768,256]{1,2,0:T(8,128)(2,1)} copy(bf16[48,768,256]{2,1,0:T(8,128)(2,1)} %all-gather.5.cloned.1.call-done) | data formatting | bytes 37748736
  515.2 13.5 %multiply_reduce_fusion = f32[24,768,8,32]{1,3,2,0:T(8,128)S(1)} fusion(bf16[24,768,8,2,32]{1,4,2,0,3:T(8,128)(2,1)} %bitcast.171, f32[24,768,8,2]{1,2,3,0:T(8,128)S(1)} %get-tuple-element.6), kind=kLoop, calls=%fused_computation | loop fusion | flops 23592960 | bytes 38928384 | tf_op jit(solution)/shard_map/nmlhw,nlwhe->mlwhe/dot_general | solution.py:88
  528.8 4.8 divide_convert_fusion
  533.6 0.0 copy-done
  533.6 20.6 %convert_reduce_fusion = (f32[24,768]{1,0:T(8,128)S(1)}, bf16[1,24,768,256]{2,3,1,0:T(8,128)(2,1)}) fusion(bf16[24,768,256]{1,2,0:T(8,128)(2,1)} %bitcast.172, bf16[256,256]{1,0:T(8,128)(2,1)S(1)} %copy-done, bf16[1,24,768,256]{2,3,1,0:T(8,128)(2,1)} %copy.142), kind=kOutput, calls=%fused_computation.4 | convolution fusion | flops 2439493632 | bytes 28516352 | tf_op jit(solution)/shard_map/dot_general | solution.py:117
  554.2 0.0 copy-start.3
  554.2 0.0 copy-start.12
  554.2 6.4 fusion.4
  560.6 0.0 copy-done.3
  560.6 0.0 copy-done.12
  560.6 10.8 fusion.15
  571.4 7.6 multiply_convert_fusion
  579.0 39.1 %copy.160 = bf16[1,24,2,384,256]{4,2,1,0,3:T(2,128)(2,1)} copy(bf16[1,24,2,384,256]{4,3,2,1,0:T(8,128)(2,1)S(1)} %multiply_convert_fusion) | data formatting | bytes 18874368 | tf_op jit(solution)/shard_map/convert_element_type | solution.py:127
  618.1 6.6 all-to-all-start
  624.8 0.0 copy-done.5
  624.8 0.1 copy.156
  624.9 0.0 copy-done.6
  624.9 0.1 copy.153
  625.2 0.9 fusion.78
  626.1 0.9 negate_convert_fusion
  627.0 202.5 %all-to-all-done = bf16[1,24,2,384,256]{4,2,1,0,3:T(2,128)(2,1)} async-done(((bf16[1,24,2,384,256]{4,2,1,0,3:T(2,128)(2,1)}), bf16[1,24,2,384,256]{4,2,1,0,3:T(2,128)(2,1)}, u32[]{:S(2)}, u32[]{:S(2)}) %all-to-all-start) | async-done | bytes 9437216 | tf_op jit(solution)/shard_map/all_to_all | solution.py:135
  829.6 10.7 copy.161
  840.3 8.3 copy.162
  848.6 19.5 %bitcast_convert_fusion.2 = bf16[24,256,2,128]{3,1,2,0:T(8,128)(2,1)S(1)} fusion(bf16[384,2,24,256,1]{3,2,1,0,4:T(8,128)(2,1)} %bitcast.178, bf16[1,128,2,384]{3,1,2,0:T(8,128)(2,1)S(1)} %get-tuple-element.14, bf16[1,128,2,384]{3,1,2,0:T(8,128)(2,1)S(1)} %get-tuple-element.13), kind=kOutput, calls=%fused_computation.40 | convolution fusion | flops 2418278400 | bytes 12976128 | tf_op jit(solution)/shard_map/pqrj,mjrkd->mpqkd/dot_general | solution.py:132
  868.1 1.0 fusion.28
  869.1 1.0 fusion.29
  870.1 1.0 copy.166
  871.1 5.3 fusion.12
  876.4 24.0 %copy.168 = bf16[1,384,2,24,256]{4,2,3,0,1:T(2,128)(2,1)} copy(bf16[1,384,2,24,256]{1,4,2,3,0:T(8,128)(2,1)} %fusion.12) | data formatting | bytes 18874368 | tf_op jit(solution)/shard_map/convert_element_type | solution.py:142
  900.3 5.2 all-to-all-start.1
  905.5 5.1 multiply_convert_fusion.4
  910.6 199.5 %all-to-all-done.1 = bf16[1,384,2,24,256]{4,2,3,0,1:T(2,128)(2,1)} async-done(((bf16[1,384,2,24,256]{4,2,3,0,1:T(2,128)(2,1)}), bf16[1,384,2,24,256]{4,2,3,0,1:T(2,128)(2,1)}, u32[]{:S(2)}, u32[]{:S(2)}) %all-to-all-start.1) | async-done | bytes 9437216 | tf_op jit(solution)/shard_map/all_to_all | solution.py:143
  1110.2 8.9 copy.169
  1119.1 8.6 copy.170
  1127.7 0.0 copy-done.7
  1127.7 15.6 %fusion.11 = bf16[1,24,768,256]{2,3,1,0:T(8,128)(2,1)} fusion(bf16[1,24,768,256]{2,3,1,0:T(8,128)(2,1)} %get-tuple-element.26, bf16[24,2,384,256]{3,2,1,0:T(8,128)(2,1)} %bitcast.177, bf16[24,384]{1,0:T(8,128)(2,1)S(1)} %copy-done.7, bf16[1,384,768]{1,2,0:T(8,128)(2,1)S(1)} %get-tuple-element.16, bf16[1,384,768]{1,2,0:T(8,128)(2,1)S(1)} %get-tuple-element.15), kind=kOutput, calls=%fused_computation.19 | convolution fusion | flops 7283146752 | bytes 29509632 | tf_op jit(solution)/shard_map/mjrkd,rkx->mjxd/dot_general | solution.py:145
  1143.3 12.6 %copy.172 = bf16[1,24,768,256]{3,2,1,0:T(8,128)(2,1)} copy(bf16[1,24,768,256]{2,3,1,0:T(8,128)(2,1)} %fusion.11) | data formatting | bytes 18874368 | tf_op jit(solution)/shard_map/convert_element_type | solution.py:151
  1155.8 0.0 copy-done.1
  (21 shorter events, 0.2 us)
Async XLA Ops:
  6.5 527.0 %copy-start = (bf16[256,256]{1,0:T(8,128)(2,1)S(1)}, bf16[256,256]{1,0:T(8,128)(2,1)}, u32[]{:S(2)}) copy-start(bf16[256,256]{1,0:T(8,128)(2,1)} %param.16) | copy-start | bytes 393220
  6.5 258.1 %all-gather.7.cloned.1.call-start = ((), (), s32[]{:S(2)}) async-start(), calls=%async_computation.3 | async-start | bytes 28311552 | tf_op jit(solution)/shard_map/all_gather | solution.py:108
  19.2 6.4 copy-start.2
  19.2 9.0 copy-start.8
  19.2 9.0 copy-start.10
  39.2 0.9 copy-start.11
  39.2 451.4 %all-gather.5.cloned.1.call-start = ((), (), s32[]{:S(2)}) async-start(), calls=%async_computation.2 | async-start | bytes 28311552 | tf_op jit(solution)/shard_map/all_gather | solution.py:114
  53.8 5.3 copy-start.9
  53.8 6.0 copy-start.4
  554.2 6.5 copy-start.3
  554.2 6.5 copy-start.12
  618.1 6.6 copy-start.5
  618.1 6.8 copy-start.6
  618.1 211.5 %all-to-all-start = ((bf16[1,24,2,384,256]{4,2,1,0,3:T(2,128)(2,1)}), bf16[1,24,2,384,256]{4,2,1,0,3:T(2,128)(2,1)}, u32[]{:S(2)}, u32[]{:S(2)}) async-start(bf16[1,24,2,384,256]{4,2,1,0,3:T(2,128)(2,1)} %copy.160), calls=%async_computation | async-start | bytes 18874368 | tf_op jit(solution)/shard_map/all_to_all | solution.py:135
  900.3 209.9 %all-to-all-start.1 = ((bf16[1,384,2,24,256]{4,2,3,0,1:T(2,128)(2,1)}), bf16[1,384,2,24,256]{4,2,3,0,1:T(2,128)(2,1)}, u32[]{:S(2)}, u32[]{:S(2)}) async-start(bf16[1,384,2,24,256]{4,2,3,0,1:T(2,128)(2,1)} %copy.168), calls=%async_computation.1 | async-start | bytes 18874368 | tf_op jit(solution)/shard_map/all_to_all | solution.py:143
  1119.1 8.6 copy-start.7
  1127.7 28.1 %copy-start.1 = (bf16[256,256]{1,0:T(8,128)(2,1)S(1)}, bf16[256,256]{1,0:T(8,128)(2,1)}, u32[]{:S(2)}) copy-start(bf16[256,256]{1,0:T(8,128)(2,1)} %param.16) | copy-start | bytes 393220
Sparse Core Ops, SparseCore 0:
  39.3 225.2 all-gather.6
  266.2 224.3 all-gather.4
where the time goes:
time: 1170 us; the launch traced here: 1160 us
  waiting for transfers between devices  775 us (66%)
  local copies, waits for them, and re-layouts  177 us (15%)
  matrix products  114 us (10%)
  other arithmetic  71.3 us (6%)
  between operations  14.1 us (1%)
  starting transfers between devices  11.8 us (1%)
    all_to_all x1, waiting for transfers between devices, shards(): lax.all_to_all(spectrum, 'grid', split_axis=3, concat_axis=1, tiled=True)  203 us
    all_to_all x1, waiting for transfers between devices, shards(): lax.all_to_all(back_rows, 'grid', split_axis=1, concat_axis=3, tiled=True)  200 us
    all_gather x1, waiting for transfers between devices, shards(): key_rows = lax.all_gather(own_keys, 'ens', axis=0, tiled=True)  190 us
    all_gather x1, waiting for transfers between devices, shards(): all_values = lax.all_gather(own_values, 'ens', axis=0, tiled=True)  184 us
    unnamed x31, local copies, waits for them, and re-layouts  63.8 us
    convert_element_type x1, local copies, waits for them, and re-layouts, shards(): (spectrum * retained[None, :, None, :, None]).astype(jnp.bfloat16)  39.1 us
    convert_element_type x1, local copies, waits for them, and re-layouts, shards(): back_rows = jnp.einsum('rpjq,mpqkd->mjrkd', inverse, second, preferred_el...  24 us
  transfers between devices with their start and end apart: 4, of which 4 were waited for; matrix products, arithmetic and copies ran while one was open for 7% of the time, Pallas kernels for 0%

commit v1 on v0

--- a/solution.py
+++ b/solution.py
@@ -140,7 +140,9 @@
     back_rows = jnp.einsum(
         "rpjq,mpqkd->mjrkd", inverse, second, preferred_element_type=jnp.float32
     ).astype(jnp.bfloat16)
-    returned = lax.all_to_all(back_rows, "grid", split_axis=1, concat_axis=3, tiled=True)
+    parts = jnp.split(back_rows, lax.axis_size("grid"), axis=1)
+    incoming = lax.all_to_all(jnp.stack(parts), "grid", 0, 0)
+    returned = jnp.concatenate(incoming, axis=3)
     returned = returned * retained.astype(jnp.bfloat16)[None, :, None, :, None]
     field_out = jnp.einsum(
         "mjrkd,rkx->mjxd",

time: 1170 us -> 1250 us (1.068)
  local copies, waits for them, and re-layouts: 177 us -> 267 us
    another operation x0 -> x18, local copies, waits for them, and re-layouts: none -> 100 us  [shards(): incoming = lax.all_to_all(jnp.stack(parts), 'grid', 0, 0)]
    convert_element_type x1 -> x0, local copies, waits for them, and re-layouts: 24 us -> none  [shards(): back_rows = jnp.einsum('rpjq,mpqkd->mjrkd', inverse, second, preferred_el...]
    unnamed x31 -> x62, local copies, waits for them, and re-layouts: 63.8 us -> 86.5 us
where the time goes in v1:
time: 1250 us; the launch traced here: 1240 us
  waiting for transfers between devices  774 us (62%)
  local copies, waits for them, and re-layouts  267 us (21%)
  matrix products  104 us (8%)
  other arithmetic  71.1 us (6%)
  between operations  14 us (1%)
    all_to_all x1, waiting for transfers between devices, shards(): lax.all_to_all(spectrum, 'grid', split_axis=3, concat_axis=1, tiled=True)  203 us
    all_to_all x1, waiting for transfers between devices, shards(): incoming = lax.all_to_all(jnp.stack(parts), 'grid', 0, 0)  200 us
    all_gather x1, waiting for transfers between devices, shards(): key_rows = lax.all_gather(own_keys, 'ens', axis=0, tiled=True)  190 us
    all_gather x1, waiting for transfers between devices, shards(): all_values = lax.all_gather(own_values, 'ens', axis=0, tiled=True)  182 us
    another operation x18, local copies, waits for them, and re-layouts, shards(): incoming = lax.all_to_all(jnp.stack(parts), 'grid', 0, 0)  100 us
    unnamed x62, local copies, waits for them, and re-layouts  86.5 us
    convert_element_type x1, local copies, waits for them, and re-layouts, shards(): (spectrum * retained[None, :, None, :, None]).astype(jnp.bfloat16)  39.1 us
  transfers between devices with their start and end apart: 4, of which 4 were waited for; matrix products, arithmetic and copies ran while one was open for 7% of the time, Pallas kernels for 0%

profile of v1, /device:TPU:11, one launch (start us, length us, event | category | flops | bytes accessed | tf_op | source)
XLA Modules:
  0.0 1241.9 jit_solution(271179578393088333)
XLA Ops:
  6.5 12.6 %copy.212 = bf16[1,24,768,256]{2,3,1,0:T(8,128)(2,1)} copy(bf16[1,24,768,256]{3,2,1,0:T(8,128)(2,1)} %param.10) | data formatting | bytes 18874368 | tf_op args[0]
  19.2 5.2 convert_reduce_fusion.1
  24.4 1.2 copy-done.2
  25.5 2.6 fusion.7
  28.2 11.0 convolution_convert_fusion.1
  40.1 13.7 %convolution_convert_fusion.2 = bf16[24,768,256]{2,1,0:T(8,128)(2,1)} fusion(bf16[256,256]{1,0:T(8,128)(2,1)S(1)} %copy-done.19, bf16[1,24,768,256]{2,3,1,0:T(8,128)(2,1)} %copy.212, f32[256]{0:T(256)S(1)} %copy-done.16, f32[24,768]{1,0:T(8,128)S(1)} %add_rsqrt_fusion.1, f32[24,768]{1,0:T(8,128)S(1)} %broadcast_multiply_fusion.1), kind=kOutput, calls=%fused_computation.36 | convolution fusion | flops 2444230656 | bytes 19153920 | tf_op jit(solution)/shard_map/dot_general | solution.py:107
  53.8 5.2 multiply_convert_fusion.1
  59.7 15.2 %bitcast_convert_fusion.3 = f32[24,8,768,32]{2,3,1,0:T(8,128)} fusion(bf16[256,256]{1,0:T(8,128)(2,1)S(1)} %copy-done.12, bf16[1,24,768,256]{2,3,1,0:T(8,128)(2,1)} %copy.212, f32[256]{0:T(256)S(1)} %copy-done.16, f32[24,768]{1,0:T(8,128)S(1)} %add_rsqrt_fusion.1, f32[24,768]{1,0:T(8,128)S(1)} %broadcast_multiply_fusion.1), kind=kOutput, calls=%fused_computation.175 | convolution fusion | flops 2448949248 | bytes 28591104 | tf_op jit(solution)/shard_map/dot_general | solution.py:104
  74.9 189.7 %all-gather.7.cloned.1.call-done = bf16[48,768,256]{2,1,0:T(8,128)(2,1)} async-done(((bf16[24,768,256]{2,1,0:T(8,128)(2,1)}), bf16[48,768,256]{2,1,0:T(8,128)(2,1)}) %all-gather.7.cloned.1.call-update) | async-done | bytes 18874384 | tf_op jit(solution)/shard_map/all_gather | solution.py:108
  264.7 25.7 %copy.291 = bf16[48,768,256]{1,2,0:T(8,128)(2,1)} copy(bf16[48,768,256]{2,1,0:T(8,128)(2,1)} %all-gather.7.cloned.1.call-done) | data formatting | bytes 37748736
  290.3 17.7 %multiply_reduce_fusion.1 = f32[24,8,768,2]{2,1,0,3:T(8,128)S(1)} fusion(bf16[24,8,768,32,2]{2,3,1,0,4:T(8,128)(2,1)} %bitcast.201, f32[24,8,768,32]{2,3,1,0:T(8,128)} %bitcast_convert_fusion.3), kind=kLoop, calls=%fused_computation.1 | loop fusion | flops 28016640 | bytes 38928384
  308.4 182.2 %all-gather.5.cloned.1.call-done = bf16[48,768,256]{2,1,0:T(8,128)(2,1)} async-done(((bf16[24,768,256]{2,1,0:T(8,128)(2,1)}), bf16[48,768,256]{2,1,0:T(8,128)(2,1)}) %all-gather.5.cloned.1.call-update) | async-done | bytes 18874384 | tf_op jit(solution)/shard_map/all_gather | solution.py:114
  490.6 24.2 %copy.290 = bf16[48,768,256]{1,2,0:T(8,128)(2,1)} copy(bf16[48,768,256]{2,1,0:T(8,128)(2,1)} %all-gather.5.cloned.1.call-done) | data formatting | bytes 37748736
  514.8 13.5 %multiply_reduce_fusion = f32[24,768,8,32]{1,3,2,0:T(8,128)S(1)} fusion(bf16[24,768,8,2,32]{1,4,2,0,3:T(8,128)(2,1)} %bitcast.202, f32[24,768,8,2]{1,2,3,0:T(8,128)S(1)} %get-tuple-element.22), kind=kLoop, calls=%fused_computation | loop fusion | flops 23592960 | bytes 38928384 | tf_op jit(solution)/shard_map/nmlhw,nlwhe->mlwhe/dot_general | solution.py:88
  528.4 4.8 divide_convert_fusion
  533.2 11.1 convert_reduce_fusion
  544.3 6.4 fusion.4
  550.7 10.8 fusion.15
  561.5 7.6 multiply_convert_fusion
  569.1 39.1 %copy.230 = bf16[1,24,2,384,256]{4,2,1,0,3:T(2,128)(2,1)} copy(bf16[1,24,2,384,256]{4,3,2,1,0:T(8,128)(2,1)S(1)} %multiply_convert_fusion) | data formatting | bytes 18874368 | tf_op jit(solution)/shard_map/convert_element_type | solution.py:127
  608.2 6.6 all-to-all-start
  616.2 0.9 fusion.78
  617.1 202.5 %all-to-all-done = bf16[1,24,2,384,256]{4,2,1,0,3:T(2,128)(2,1)} async-done(((bf16[1,24,2,384,256]{4,2,1,0,3:T(2,128)(2,1)}), bf16[1,24,2,384,256]{4,2,1,0,3:T(2,128)(2,1)}, u32[]{:S(2)}, u32[]{:S(2)}) %all-to-all-start) | async-done | bytes 9437216 | tf_op jit(solution)/shard_map/all_to_all | solution.py:135
  819.7 10.8 copy.231
  830.4 8.3 copy.232
  838.7 19.7 %bitcast_convert_fusion.2 = bf16[24,256,2,128]{3,1,2,0:T(8,128)(2,1)S(1)} fusion(bf16[384,2,24,256,1]{3,2,1,0,4:T(8,128)(2,1)} %bitcast.208, bf16[1,128,2,384]{3,1,2,0:T(8,128)(2,1)S(1)} %get-tuple-element.30, bf16[1,128,2,384]{3,1,2,0:T(8,128)(2,1)S(1)} %get-tuple-element.29), kind=kOutput, calls=%fused_computation.40 | convolution fusion | flops 2418278400 | bytes 12976128 | tf_op jit(solution)/shard_map/pqrj,mjrkd->mpqkd/dot_general | solution.py:132
  858.4 1.0 fusion.28
  859.5 1.0 fusion.29
  860.5 1.0 copy.236
  861.5 5.1 fusion.12
  866.6 35.9 %slice_bitcast_fusion = (bf16[1,1,24,2,24,256]{2,5,3,4,1,0:T(8,128)(2,1)}, bf16[1,1,24,2,24,256]{2,5,3,4,1,0:T(8,128)(2,1)}, bf16[1,1,24,2,24,256]{2,5,3,4,1,0:T...) fusion(bf16[1,384,2,24,256]{1,4,2,3,0:T(8,128)(2,1)} %fusion.12), kind=kLoop, calls=%fused_computation.44 | loop fusion | bytes 18874368 | tf_op jit(solution)/shard_map/stack | solution.py:144
  902.5 4.1 copy.253
  906.5 4.0 copy.252
  910.6 4.1 copy.251
  914.6 4.1 copy.250
  918.7 4.1 copy.249
  922.8 4.1 copy.248
  926.8 4.1 copy.247
  930.9 4.1 copy.246
  934.9 4.1 copy.245
  939.0 4.0 copy.244
  943.1 4.1 copy.243
  947.1 4.0 copy.242
  951.2 4.0 copy.241
  955.2 4.0 copy.240
  959.2 4.0 copy.239
  963.3 2.4 copy.238
  965.7 2.1 constant_dynamic-update-slice_fusion.15
  967.8 1.9 constant_dynamic-update-slice_fusion.14
  969.7 1.9 constant_dynamic-update-slice_fusion.13
  971.6 1.9 constant_dynamic-update-slice_fusion.12
  973.6 1.9 constant_dynamic-update-slice_fusion.11
  975.5 1.9 constant_dynamic-update-slice_fusion.10
  977.4 1.9 constant_dynamic-update-slice_fusion.9
  979.4 1.9 constant_dynamic-update-slice_fusion.8
  983.9 0.9 constant_dynamic-update-slice_fusion.4
  985.6 0.9 constant_dynamic-update-slice_fusion.2
  986.5 0.9 constant_dynamic-update-slice_fusion.1
  988.3 5.1 all-to-all-start.1
  993.4 5.1 multiply_convert_fusion.4
  998.6 199.5 %all-to-all-done.1 = bf16[16,1,24,2,24,256]{5,4,3,2,1,0:T(8,128)(2,1)} async-done(((bf16[16,1,24,2,24,256]{5,4,3,2,1,0:T(8,128)(2,1)}), bf16[16,1,24,2,24,256]{5,4,3,2,1,0:T(8,128)(2,1)}, u32[]{:S(2)}, u32[]{:S(2)}) %all-to-all-start.1) | async-done | bytes 9437216 | tf_op jit(solution)/shard_map/all_to_all | solution.py:144
  1198.1 8.6 copy.254
  1206.7 15.6 %fusion.11 = bf16[1,24,768,256]{2,3,1,0:T(8,128)(2,1)} fusion(bf16[1,24,768,256]{2,3,1,0:T(8,128)(2,1)} %get-tuple-element.42, bf16[24,2,384,256]{3,2,1,0:T(8,128)(2,1)} %bitcast.207, bf16[24,384]{1,0:T(8,128)(2,1)S(1)} %copy-done.15, bf16[1,384,768]{1,2,0:T(8,128)(2,1)S(1)} %get-tuple-element.32, bf16[1,384,768]{1,2,0:T(8,128)(2,1)S(1)} %get-tuple-element.31), kind=kOutput, calls=%fused_computation.19 | convolution fusion | flops 7283146752 | bytes 29509632 | tf_op jit(solution)/shard_map/mjrkd,rkx->mjxd/dot_general | solution.py:147
  1222.2 12.6 %copy.256 = bf16[1,24,768,256]{3,2,1,0:T(8,128)(2,1)} copy(bf16[1,24,768,256]{2,3,1,0:T(8,128)(2,1)} %fusion.11) | data formatting | bytes 18874368 | tf_op jit(solution)/shard_map/convert_element_type | solution.py:153
  (68 shorter events, 7.6 us)
Async XLA Ops:
  6.5 526.6 %copy-start = (bf16[256,256]{1,0:T(8,128)(2,1)S(1)}, bf16[256,256]{1,0:T(8,128)(2,1)}, u32[]{:S(2)}) copy-start(bf16[256,256]{1,0:T(8,128)(2,1)} %param.16) | copy-start | bytes 393220
  6.5 258.1 %all-gather.7.cloned.1.call-start = ((), (), s32[]{:S(2)}) async-start(), calls=%async_computation.3 | async-start | bytes 28311552 | tf_op jit(solution)/shard_map/all_gather | solution.py:108
  19.2 6.4 copy-start.2
  19.2 9.0 copy-start.16
  19.2 9.0 copy-start.18
  39.2 0.9 copy-start.19
  39.2 451.4 %all-gather.5.cloned.1.call-start = ((), (), s32[]{:S(2)}) async-start(), calls=%async_computation.2 | async-start | bytes 28311552 | tf_op jit(solution)/shard_map/all_gather | solution.py:114
  53.8 5.2 copy-start.17
  53.8 5.9 copy-start.12
  544.2 6.5 copy-start.3
  544.2 6.5 copy-start.20
  608.2 6.6 copy-start.13
  608.2 6.8 copy-start.14
  608.2 211.5 %all-to-all-start = ((bf16[1,24,2,384,256]{4,2,1,0,3:T(2,128)(2,1)}), bf16[1,24,2,384,256]{4,2,1,0,3:T(2,128)(2,1)}, u32[]{:S(2)}, u32[]{:S(2)}) async-start(bf16[1,24,2,384,256]{4,2,1,0,3:T(2,128)(2,1)} %copy.230), calls=%async_computation | async-start | bytes 18874368 | tf_op jit(solution)/shard_map/all_to_all | solution.py:135
  965.7 15.6 %copy-start.11 = (bf16[1,1,24,2,24,256]{5,4,3,2,1,0:T(8,128)(2,1)S(1)}, bf16[1,1,24,2,24,256]{5,4,3,2,1,0:T(8,128)(2,1)}, u32[]{:S(2)}) copy-start(bf16[1,1,24,2,24,256]{5,4,3,2,1,0:T(8,128)(2,1)} %copy.246) | copy-start | bytes 1769476
  965.7 16.5 %copy-start.10 = (bf16[1,1,24,2,24,256]{5,4,3,2,1,0:T(8,128)(2,1)S(1)}, bf16[1,1,24,2,24,256]{5,4,3,2,1,0:T(8,128)(2,1)}, u32[]{:S(2)}) copy-start(bf16[1,1,24,2,24,256]{5,4,3,2,1,0:T(8,128)(2,1)} %copy.247) | copy-start | bytes 1769476
  965.7 17.3 %copy-start.9 = (bf16[1,1,24,2,24,256]{5,4,3,2,1,0:T(8,128)(2,1)S(1)}, bf16[1,1,24,2,24,256]{5,4,3,2,1,0:T(8,128)(2,1)}, u32[]{:S(2)}) copy-start(bf16[1,1,24,2,24,256]{5,4,3,2,1,0:T(8,128)(2,1)} %copy.248) | copy-start | bytes 1769476
  965.7 18.2 %copy-start.8 = (bf16[1,1,24,2,24,256]{5,4,3,2,1,0:T(8,128)(2,1)S(1)}, bf16[1,1,24,2,24,256]{5,4,3,2,1,0:T(8,128)(2,1)}, u32[]{:S(2)}) copy-start(bf16[1,1,24,2,24,256]{5,4,3,2,1,0:T(8,128)(2,1)} %copy.249) | copy-start | bytes 1769476
  965.7 19.1 %copy-start.7 = (bf16[1,1,24,2,24,256]{5,4,3,2,1,0:T(8,128)(2,1)S(1)}, bf16[1,1,24,2,24,256]{5,4,3,2,1,0:T(8,128)(2,1)}, u32[]{:S(2)}) copy-start(bf16[1,1,24,2,24,256]{5,4,3,2,1,0:T(8,128)(2,1)} %copy.250) | copy-start | bytes 1769476
  965.7 19.9 %copy-start.6 = (bf16[1,1,24,2,24,256]{5,4,3,2,1,0:T(8,128)(2,1)S(1)}, bf16[1,1,24,2,24,256]{5,4,3,2,1,0:T(8,128)(2,1)}, u32[]{:S(2)}) copy-start(bf16[1,1,24,2,24,256]{5,4,3,2,1,0:T(8,128)(2,1)} %copy.251) | copy-start | bytes 1769476
  965.7 20.8 %copy-start.5 = (bf16[1,1,24,2,24,256]{5,4,3,2,1,0:T(8,128)(2,1)S(1)}, bf16[1,1,24,2,24,256]{5,4,3,2,1,0:T(8,128)(2,1)}, u32[]{:S(2)}) copy-start(bf16[1,1,24,2,24,256]{5,4,3,2,1,0:T(8,128)(2,1)} %copy.252) | copy-start | bytes 1769476
  965.7 21.7 %copy-start.4 = (bf16[1,1,24,2,24,256]{5,4,3,2,1,0:T(8,128)(2,1)S(1)}, bf16[1,1,24,2,24,256]{5,4,3,2,1,0:T(8,128)(2,1)}, u32[]{:S(2)}) copy-start(bf16[1,1,24,2,24,256]{5,4,3,2,1,0:T(8,128)(2,1)} %copy.253) | copy-start | bytes 1769476
  988.3 209.8 %all-to-all-start.1 = ((bf16[16,1,24,2,24,256]{5,4,3,2,1,0:T(8,128)(2,1)}), bf16[16,1,24,2,24,256]{5,4,3,2,1,0:T(8,128)(2,1)}, u32[]{:S(2)}, u32[]{:S(2)}) async-start(bf16[16,1,24,2,24,256]{5,4,3,2,1,0:T(8,128)(2,1)} %constant_dynamic-update-slice_fusion), calls=%async_computation.1 | async-start | bytes 18874368 | tf_op jit(solution)/shard_map/all_to_all | solution.py:144
  998.5 208.1 %copy-start.15 = (bf16[24,384]{1,0:T(8,128)(2,1)S(1)}, bf16[24,384]{1,0:T(8,128)(2,1)}, u32[]{:S(2)}) copy-start(bf16[24,384]{1,0:T(8,128)(2,1)} %get-tuple-element.33) | copy-start | bytes 55300
  1206.7 28.2 %copy-start.1 = (bf16[256,256]{1,0:T(8,128)(2,1)S(1)}, bf16[256,256]{1,0:T(8,128)(2,1)}, u32[]{:S(2)}) copy-start(bf16[256,256]{1,0:T(8,128)(2,1)} %param.16) | copy-start | bytes 393220
Sparse Core Ops, SparseCore 0:
  39.3 225.2 all-gather.6
  266.2 224.3 all-gather.4
